TPU v7x, 32 devices: a whole 2x2x4 slice. The times are simulated.
32 devices in a mesh: dp: 2 (over y), row: 4 (over x, core), col: 4 (over z).
Axes of the slice: x: 2, y: 2, z: 4, core: 2. Of those that a mesh axis runs over, the one named last changes fastest.
Arguments:
- grad_out: bfloat16 [512, 8192], P(('dp', 'col'), 'row'), may hold values from -6 to 6
- saved_hidden: bfloat16 [512, 26624], P(('dp', 'row'), 'col'), may hold values from -0.26367188 to 0.26367188
- down_weight: bfloat16 [26624, 8192], P('col', 'row'), may hold values from -0.0625 to 0.0625
Outputs:
- input_grad: bfloat16 [512, 26624], P(('dp', 'row'), 'col')
- weight_grad: bfloat16 [26624, 8192], P(('col', 'dp'), 'row')
All inputs are finite; a program needn't handle non-finite values.
Results may differ from a plain program's by a relative error of at most 0.001.
Values may be sent and summed in bfloat16 or wider, within the bound.
No kernel may reach another device: no remote copies, remote signals or barrier semaphores. Data moves between devices by JAX's collectives and lax.ppermute only.
A program may use at most 128 MiB of HBM per device.

v0:
```python
import jax
import jax.numpy as jnp
from jax import lax
from jax.sharding import PartitionSpec as P


def local(grad_out, saved_hidden, down_weight):
    local_rows = saved_hidden.shape[0]
    gathered_all = lax.all_gather(grad_out, ("dp", "col"), axis=0, tiled=True)
    copy_count = lax.axis_size("dp")
    row_count = lax.axis_size("row")
    copy_rows = gathered_all.shape[0] // copy_count
    grad_copy = lax.dynamic_slice_in_dim(
        gathered_all, lax.axis_index("dp") * copy_rows, copy_rows, 0
    )
    hidden_parts = lax.all_to_all(saved_hidden, "dp", split_axis=1, concat_axis=0, tiled=True)
    hidden_stack = lax.all_gather(hidden_parts, "row", axis=0, tiled=True)
    hidden_grid = hidden_stack.reshape(row_count, copy_count, local_rows, hidden_stack.shape[1])
    grad_grid = gathered_all.reshape(copy_count, row_count, local_rows, gathered_all.shape[1])
    weight_grad = jnp.einsum(
        "rdtk,drtn->kn", hidden_grid, grad_grid, preferred_element_type=jnp.float32
    )
    input_grad = lax.psum_scatter(
        lax.dot_general(
            grad_copy, down_weight, (((1,), (1,)), ((), ())), preferred_element_type=jnp.float32
        ),
        "row",
        scatter_dimension=0,
        tiled=True,
    )
    return (input_grad.astype(jnp.bfloat16), weight_grad.astype(jnp.bfloat16))


def solution(mesh):
    placed = (P(("dp", "col"), "row"), P(("dp", "row"), "col"), P("col", "row"))
    return jax.shard_map(
        local,
        mesh=mesh,
        in_specs=placed,
        out_specs=(P(("dp", "row"), "col"), P(("col", "dp"), "row")),
        check_vma=False,
    )
```

profile of v0, /device:TPU:0, one launch (start us, length us, event | category | flops | bytes accessed | tf_op | source)
XLA Modules:
  0.0 167.5 jit_solution(16563208441328073580)
XLA Ops:
  7.2 0.0 all-gather.3.cloned.1.call-start
  7.2 0.7 all-gather.3.cloned.1.call-update
  7.9 0.0 all-gather.5.cloned.1.call-start
  7.9 1.2 copy.15
  9.2 18.8 %all_to_all.19 = bf16[64,2,3328]{2,0,1:T(8,128)(2,1)} all-to-all(bf16[64,2,3328]{2,0,1:T(8,128)(2,1)S(1)} %bitcast.16), channel_id=1, replica_groups=mesh['dp'=2,'row'=4,'col'=4] {'dp'}, dimensions={1} | all-to-all | bytes 1703936 | tf_op jit(solution)/shard_map/all_to_all | solution.py:16
  28.0 0.0 all-gather.5.cloned.1.call-update
  28.0 0.0 reduce-scatter.2.cloned.1.call-start
  28.1 35.4 %all-gather.3.cloned.1.call-done = bf16[512,2048]{1,0:T(8,128)(2,1)} async-done(((bf16[64,2048]{1,0:T(8,128)(2,1)}), bf16[512,2048]{1,0:T(8,128)(2,1)}) %all-gather.3.cloned.1.call-update) | async-done | bytes 2097168 | tf_op jit(solution)/shard_map/all_gather | solution.py:9
  63.5 16.8 %fusion.1 = f32[256,6656]{1,0:T(8,128)} fusion(bf16[6656,2048]{1,0:T(8,128)(2,1)} %param.5, bf16[512,2048]{1,0:T(8,128)(2,1)} %all-gather.3.cloned.1.call-done, s32[]{:T(128)S(6)} %select_n.3), kind=kOutput, calls=%fused_computation.2 | convolution fusion | flops 6979321856 | bytes 35127300 | tf_op jit(solution)/shard_map/dot_general | solution.py:24
  80.2 0.0 copy-start
  80.2 0.0 reduce-scatter.2.cloned.1.call-update
  80.3 13.3 %all-gather.5.cloned.1.call-done = bf16[512,3328]{1,0:T(8,128)(2,1)} async-done(((bf16[128,3328]{1,0:T(8,128)(2,1)}), bf16[512,3328]{1,0:T(8,128)(2,1)}) %all-gather.5.cloned.1.call-update) | async-done | bytes 3407888 | tf_op jit(solution)/shard_map/all_gather | solution.py:17
  93.6 0.0 copy-done
  93.6 13.3 %bitcast_convert_fusion = bf16[3328,2048]{1,0:T(8,128)(2,1)} fusion(bf16[2,4,64,2048]{3,2,1,0:T(8,128)(2,1)S(1)} %bitcast.19, bf16[4,2,64,3328]{3,2,1,0:T(8,128)(2,1)} %bitcast.18), kind=kOutput, calls=%fused_computation | convolution fusion | flops 6986137600 | bytes 19136512 | tf_op jit(solution)/shard_map/rdtk,drtn->kn/dot_general | solution.py:20
  106.9 51.6 %reduce-scatter.2.cloned.1.call-done = f32[64,6656]{1,0:T(8,128)} async-done(((f32[256,6656]{1,0:T(8,128)}), f32[64,6656]{1,0:T(8,128)}) %reduce-scatter.2.cloned.1.call-update) | async-done | bytes 1703952 | tf_op jit(solution)/shard_map/reduce_scatter | solution.py:23
  158.6 2.4 %convert_element_type.6 = bf16[64,6656]{1,0:T(8,128)(2,1)} convert(f32[64,6656]{1,0:T(8,128)} %reduce-scatter.2.cloned.1.call-done) | non-fusion elementwise | flops 425984 | bytes 2555904 | tf_op jit(solution)/shard_map/convert_element_type | solution.py:31
Async XLA Ops:
  7.2 56.3 %all-gather.3.cloned.1.call-start = ((), (), s32[]{:S(2)}) async-start(), calls=%async_computation.2 | async-start | bytes 2359296 | tf_op jit(solution)/shard_map/all_gather | solution.py:9
  7.9 85.7 %all-gather.5.cloned.1.call-start = ((), (), s32[]{:S(2)}) async-start(), calls=%async_computation.4 | async-start | bytes 4259840 | tf_op jit(solution)/shard_map/all_gather | solution.py:17
  28.0 130.6 %reduce-scatter.2.cloned.1.call-start = ((), (), s32[]{:S(2)}) async-start(), calls=%async_computation.3 | async-start | bytes 8519680 | tf_op jit(solution)/shard_map/reduce_scatter | solution.py:23
  80.2 13.4 %copy-start = (bf16[512,2048]{1,0:T(8,128)(2,1)S(1)}, bf16[512,2048]{1,0:T(8,128)(2,1)}, u32[]{:S(2)}) copy-start(bf16[512,2048]{1,0:T(8,128)(2,1)} %all-gather.3.cloned.1.call-done) | copy-start | bytes 6291460
Sparse Core Ops, SparseCore 0:
  10.1 53.3 all-gather.2
  65.0 28.5 all-gather.4
  96.1 62.3 reduce-scatter.1
where the time goes:
time: 168 us
  waiting for transfers between devices  101 us (60%)
  matrix products  30.1 us (18%)
  blocking collectives  18.8 us (11%)
  between operations  13.8 us (8%)
  other arithmetic  2.44 us (1%)
    reduce_scatter x1, waiting for transfers between devices, local(): lax.psum_scatter(lax.dot_general(grad_copy, down_weight, (((1,), (1,)), (...  51.6 us
    all_gather x1, waiting for transfers between devices, local(): gathered_all = lax.all_gather(grad_out, ('dp', 'col'), axis=0, tiled=True)  35.4 us
    all_to_all x1, blocking collectives, local(): lax.all_to_all(saved_hidden, 'dp', split_axis=1, concat_axis=0, tiled=True)  18.8 us
    dot_general x1, matrix products, local(): lax.dot_general(grad_copy, down_weight, (((1,), (1,)), ((), ())), preferr...  16.8 us
    all_gather x1, waiting for transfers between devices, local(): hidden_stack = lax.all_gather(hidden_parts, 'row', axis=0, tiled=True)  13.3 us
    dot_general x1, matrix products, local(): jnp.einsum('rdtk,drtn->kn', hidden_grid, grad_grid, preferred_element_typ...  13.3 us
  transfers between devices with their start and end apart: 3, of which 3 were waited for; matrix products, arithmetic and copies ran while one was open for 19% of the time, Pallas kernels for 0%

commit v1 on v0

--- a/solution.py
+++ b/solution.py
@@ -14,7 +14,14 @@
         gathered_all, lax.axis_index("dp") * copy_rows, copy_rows, 0
     )
     hidden_parts = lax.all_to_all(saved_hidden, "dp", split_axis=1, concat_axis=0, tiled=True)
-    hidden_stack = lax.all_gather(hidden_parts, "row", axis=0, tiled=True)
+    peers = lax.axis_size("row")
+    route = [(i, (i + 1) % peers) for i in range(peers)]
+    shards = [hidden_parts]
+    for stride in range(1, peers):
+        shards = [lax.ppermute(shards[0], "row", route), *shards]
+    whole = jnp.concatenate(shards, axis=0)
+    turn = (lax.axis_index("row") + 1) * shards[-1].shape[0]
+    hidden_stack = jnp.roll(whole, turn, axis=0)
     hidden_grid = hidden_stack.reshape(row_count, copy_count, local_rows, hidden_stack.shape[1])
     grad_grid = gathered_all.reshape(copy_count, row_count, local_rows, gathered_all.shape[1])
     weight_grad = jnp.einsum(

time: 168 us -> 180 us (1.071)
  waiting for transfers between devices: 101 us -> 119 us
  blocking collectives: 18.8 us -> 12.3 us
  matrix products: 30.1 us -> 26.1 us
  starting transfers between devices: 0.12 us -> 3.02 us
    ppermute x0 -> x3, waiting for transfers between devices: none -> 63.9 us  [local(): shards = [lax.ppermute(shards[0], 'row', route), *shards]]
    reduce_scatter x1, waiting for transfers between devices: 51.6 us -> 0.01 us  [local(): lax.psum_scatter(lax.dot_general(grad_copy, down_weight, (((1,), (1,)), (...]
    all_gather x1, waiting for transfers between devices: 35.4 us -> 54 us  [local(): gathered_all = lax.all_gather(grad_out, ('dp', 'col'), axis=0, tiled=True)]
    all_gather x1 -> x0, waiting for transfers between devices: 13.3 us -> none  [local(): hidden_stack = lax.all_gather(hidden_parts, 'row', axis=0, tiled=True)]
    all_to_all x1, blocking collectives: 18.8 us -> 12.3 us  [local(): lax.all_to_all(saved_hidden, 'dp', split_axis=1, concat_axis=0, tiled=True)]
    ppermute x0 -> x3, starting transfers between devices: none -> 2.95 us  [local(): shards = [lax.ppermute(shards[0], 'row', route), *shards]]
    dot_general x1, matrix products: 13.3 us -> 10.4 us  [local(): jnp.einsum('rdtk,drtn->kn', hidden_grid, grad_grid, preferred_element_typ...]
    unnamed x2 -> x11, local copies, waits for them, and re-layouts: 0.01 us -> 2.62 us
  transfers between devices with their start and end apart: 3 -> 5, of which waited for: 3 -> 4; matrix products, arithmetic and copies ran while one was open for 19% -> 6% of each run, Pallas kernels for 0% -> 0%
where the time goes in v1:
time: 180 us
  waiting for transfers between devices  119 us (66%)
  matrix products  26.1 us (14%)
  between operations  14.1 us (8%)
  blocking collectives  12.3 us (7%)
  starting transfers between devices  3.02 us (2%)
  local copies, waits for them, and re-layouts  2.96 us (2%)
  other arithmetic  2.44 us (1%)
    ppermute x3, waiting for transfers between devices, local(): shards = [lax.ppermute(shards[0], 'row', route), *shards]  63.9 us
    all_gather x1, waiting for transfers between devices, local(): gathered_all = lax.all_gather(grad_out, ('dp', 'col'), axis=0, tiled=True)  54 us
    dot_general x1, matrix products, local(): lax.dot_general(grad_copy, down_weight, (((1,), (1,)), ((), ())), preferr...  15.6 us
    all_to_all x1, blocking collectives, local(): lax.all_to_all(saved_hidden, 'dp', split_axis=1, concat_axis=0, tiled=True)  12.3 us
    dot_general x1, matrix products, local(): jnp.einsum('rdtk,drtn->kn', hidden_grid, grad_grid, preferred_element_typ...  10.4 us
  transfers between devices with their start and end apart: 5, of which 4 were waited for; matrix products, arithmetic and copies ran while one was open for 6% of the time, Pallas kernels for 0%

profile of v1, /device:TPU:0, one launch (start us, length us, event | category | flops | bytes accessed | tf_op | source)
XLA Modules:
  0.0 179.5 jit_solution(12486035017376318654)
XLA Ops:
  7.2 0.7 all-gather.2.cloned.1.call-update
  7.9 0.0 reduce-scatter.2.cloned.1.call-start
  7.9 54.0 %all-gather.2.cloned.1.call-done = bf16[512,2048]{1,0:T(8,128)(2,1)} async-done(((bf16[64,2048]{1,0:T(8,128)(2,1)}), bf16[512,2048]{1,0:T(8,128)(2,1)}) %all-gather.2.cloned.1.call-update) | async-done | bytes 2097168 | tf_op jit(solution)/shard_map/all_gather | solution.py:9
  61.9 15.6 %fusion.1 = f32[256,6656]{1,0:T(8,128)} fusion(bf16[6656,2048]{1,0:T(8,128)(2,1)} %param.5, bf16[512,2048]{1,0:T(8,128)(2,1)} %all-gather.2.cloned.1.call-done, s32[]{:T(128)S(6)} %select_n.16), kind=kOutput, calls=%fused_computation.2 | convolution fusion | flops 6979321856 | bytes 35127300 | tf_op jit(solution)/shard_map/dot_general | solution.py:31
  77.6 1.1 copy-done
  78.7 0.1 copy.15
  78.8 12.3 %all_to_all.19 = bf16[64,2,3328]{2,0,1:T(8,128)(2,1)S(1)} all-to-all(bf16[64,2,3328]{2,0,1:T(8,128)(2,1)S(1)} %bitcast.19), channel_id=1, replica_groups=mesh['dp'=2,'row'=4,'col'=4] {'dp'}, dimensions={1} | all-to-all | bytes 1703936 | tf_op jit(solution)/shard_map/all_to_all | solution.py:16
  91.1 17.8 %collective-permute-done = bf16[128,3328]{1,0:T(8,128)(2,1)S(1)} collective-permute-done((bf16[128,3328]{1,0:T(8,128)(2,1)S(1)}, bf16[128,3328]{1,0:T(8,128)(2,1)S(1)}, u32[]{:S(2)}, u32[]{:S(2)}) %collective-permute-start) | collective-permute-done | bytes 852000 | tf_op jit(solution)/shard_map/ppermute | solution.py:21
  108.9 1.5 collective-permute-start.1
  110.3 29.0 %collective-permute-done.1 = bf16[128,3328]{1,0:T(8,128)(2,1)S(1)} collective-permute-done((bf16[128,3328]{1,0:T(8,128)(2,1)S(1)}, bf16[128,3328]{1,0:T(8,128)(2,1)S(1)}, u32[]{:S(2)}, u32[]{:S(2)}) %collective-permute-start.1) | collective-permute-done | bytes 852000 | tf_op jit(solution)/shard_map/ppermute | solution.py:21
  139.4 1.5 collective-permute-start.2
  140.8 17.1 %collective-permute-done.2 = bf16[128,3328]{1,0:T(8,128)(2,1)S(1)} collective-permute-done((bf16[128,3328]{1,0:T(8,128)(2,1)S(1)}, bf16[128,3328]{1,0:T(8,128)(2,1)S(1)}, u32[]{:S(2)}, u32[]{:S(2)}) %collective-permute-start.2) | collective-permute-done | bytes 852000 | tf_op jit(solution)/shard_map/ppermute | solution.py:21
  158.0 0.1 constant_dynamic-update-slice_fusion.7
  158.0 0.1 constant_dynamic-update-slice_fusion.6
  158.1 0.1 constant_dynamic-update-slice_fusion.5
  158.1 0.1 constant_dynamic-update-slice_fusion.4
  158.2 0.1 constant_dynamic-update-slice_fusion.3
  158.3 0.1 constant_dynamic-update-slice_fusion.2
  158.4 0.1 constant_dynamic-update-slice_fusion.1
  158.4 0.1 constant_dynamic-update-slice_fusion
  158.5 0.2 constant_dynamic-slice_fusion
  158.7 1.1 copy-done.1
  159.8 10.4 %bitcast_convert_fusion = bf16[3328,2048]{1,0:T(8,128)(2,1)} fusion(bf16[2,4,64,2048]{3,2,1,0:T(8,128)(2,1)S(1)} %bitcast.21, bf16[4,2,64,3328]{3,2,1,0:T(8,128)(2,1)S(1)} %bitcast.18), kind=kOutput, calls=%fused_computation | convolution fusion | flops 6986137600 | bytes 19136512 | tf_op jit(solution)/shard_map/rdtk,drtn->kn/dot_general | solution.py:27
  170.3 2.4 %convert_element_type.6 = bf16[64,6656]{1,0:T(8,128)(2,1)} convert(f32[64,6656]{1,0:T(8,128)} %reduce-scatter.2.cloned.1.call-done) | non-fusion elementwise | flops 425984 | bytes 2555904 | tf_op jit(solution)/shard_map/convert_element_type | solution.py:38
  (6 shorter events, 0.1 us)
Async XLA Ops:
  7.2 54.8 %all-gather.2.cloned.1.call-start = ((), (), s32[]{:S(2)}) async-start(), calls=%async_computation.2 | async-start | bytes 2359296 | tf_op jit(solution)/shard_map/all_gather | solution.py:9
  7.9 162.4 %reduce-scatter.2.cloned.1.call-start = ((), (), s32[]{:S(2)}) async-start(), calls=%async_computation.3 | async-start | bytes 8519680 | tf_op jit(solution)/shard_map/reduce_scatter | solution.py:30
  77.6 1.2 copy-start
  91.1 17.8 %collective-permute-start = (bf16[128,3328]{1,0:T(8,128)(2,1)S(1)}, bf16[128,3328]{1,0:T(8,128)(2,1)S(1)}, u32[]{:S(2)}, u32[]{:S(2)}) collective-permute-start(bf16[128,3328]{1,0:T(8,128)(2,1)S(1)} %bitcast.15), channel_id=1, source_target_pairs={{0,4},{4,8},{8,12},{12,0},{1,5},{5,9},{9,13},{13,1},{2,6},{6,10},{... | collective-permute-start | bytes 2555912 | tf_op jit(solution)/shard_map/ppermute | solution.py:21
  108.9 30.5 %collective-permute-start.1 = (bf16[128,3328]{1,0:T(8,128)(2,1)S(1)}, bf16[128,3328]{1,0:T(8,128)(2,1)S(1)}, u32[]{:S(2)}, u32[]{:S(2)}) collective-permute-start(bf16[128,3328]{1,0:T(8,128)(2,1)S(1)} %collective-permute-done), channel_id=1, source_target_pairs={{0,4},{4,8},{8,12},{12,0},{1,5},{5,9},{9,13},{13,1},{2,6},{6,10},{... | collective-permute-start | bytes 2555912 | tf_op jit(solution)/shard_map/ppermute | solution.py:21
  139.4 18.6 %collective-permute-start.2 = (bf16[128,3328]{1,0:T(8,128)(2,1)S(1)}, bf16[128,3328]{1,0:T(8,128)(2,1)S(1)}, u32[]{:S(2)}, u32[]{:S(2)}) collective-permute-start(bf16[128,3328]{1,0:T(8,128)(2,1)S(1)} %collective-permute-done.1), channel_id=1, source_target_pairs={{0,4},{4,8},{8,12},{12,0},{1,5},{5,9},{9,13},{13,1},{2,6},{6,10},{... | collective-permute-start | bytes 2555912 | tf_op jit(solution)/shard_map/ppermute | solution.py:21
  158.2 1.6 copy-start.1
Sparse Core Ops, SparseCore 0:
  10.1 51.8 all-gather.1
  77.7 76.1 reduce-scatter.1
